TPU v7x, 32 devices: a whole 2x2x4 slice. The times are simulated.
32 devices in a mesh: dom: 8 (over z, y), sub: 4 (over x, core).
Axes of the slice: x: 2, y: 2, z: 4, core: 2. Of those that a mesh axis runs over, the one named last changes fastest.
Arguments:
- nodes: bfloat16 [16384, 128], P(('dom', 'sub')), may hold values from -6 to 6
- edges: bfloat16 [65536, 128], P(('dom', 'sub')), may hold values from -6 to 6
- senders: int32 [65536], P(('dom', 'sub')), may hold values from 0 to 895
- receivers: int32 [65536], P(('dom', 'sub')), may hold values from 0 to 511
- edge_live: int32 [65536], P(('dom', 'sub')), may hold values from 0 to 1, as said below
- outlet_flags: int32 [16384], P(('dom', 'sub')), may hold values 0 or 1
- send_rows: int32 [12288], P(('dom', 'sub')), may hold values from 0 to 511
- edge_first: float32 [3, 384, 128], replicated, may hold values from -0.3125 to 0.3125
- edge_bias: float32 [3, 128], replicated, may hold values from -3 to 3
- edge_second: float32 [3, 128, 128], replicated, may hold values from -0.5 to 0.5
- edge_offset: float32 [3, 128], replicated, may hold values from -3 to 3
- edge_gain: float32 [3, 128], replicated, may hold values from 0.25 to 1.75
- node_first: float32 [3, 256, 128], replicated, may hold values from -0.375 to 0.375
- node_bias: float32 [3, 128], replicated, may hold values from -3 to 3
- node_second: float32 [3, 128, 128], replicated, may hold values from -0.5 to 0.5
- node_offset: float32 [3, 128], replicated, may hold values from -3 to 3
- node_gain: float32 [3, 128], replicated, may hold values from 0.25 to 1.75
- outlet_map: float32 [3, 128, 128], replicated, may hold values from -0.5 to 0.5
- grad_out: float32 [16384, 128], P(('dom', 'sub')), may hold values from -6 to 6
Outputs:
- latent_out: float32 [16384, 128], P(('dom', 'sub'))
- latent_grad: float32 [16384, 128], P(('dom', 'sub'))
- edge_first_grad: float32 [3, 384, 128], replicated
- edge_bias_grad: float32 [3, 128], replicated
- edge_second_grad: float32 [3, 128, 128], replicated
- edge_offset_grad: float32 [3, 128], replicated
- edge_gain_grad: float32 [3, 128], replicated
- node_first_grad: float32 [3, 256, 128], replicated
- node_bias_grad: float32 [3, 128], replicated
- node_second_grad: float32 [3, 128, 128], replicated
- node_offset_grad: float32 [3, 128], replicated
- node_gain_grad: float32 [3, 128], replicated
- outlet_map_grad: float32 [3, 128, 128], replicated
Inputs may be any that keep to these rules, and one draw needn't show every extreme that they name: `edge_live`: on each device the live edge slots are the first ones of its 2048; each device has between a quarter and all of them live, and some device has all live. `senders`: indices below 512 name the device's own nodes; higher ones name halo rows.
All inputs are finite; a program needn't handle non-finite values. No bound on the sum of `outlet_flags` on one device may be relied on, other than what follows from the above.
Results may differ from a plain program's by a relative error of at most 0.018.
Values may be sent and summed in bfloat16 or wider, within the bound.
A program may use at most 320 MiB of HBM per device.

v0:
```python
import jax
import jax.numpy as jnp
from jax import lax
from jax.sharding import PartitionSpec as P


def passed_along(value, axis, steps):
    count = lax.axis_size(axis)
    first, last = (max(0, -steps), min(count, count - steps))
    return lax.ppermute(value, axis, [(source, source + steps) for source in range(first, last)])


def normalize(values):
    mean = jnp.mean(values, axis=-1, keepdims=True)
    centered = values - mean
    variance = jnp.mean(centered * centered, axis=-1, keepdims=True)
    return centered * lax.rsqrt(variance + 1e-05)


def layer_local(latent, edge_state, halo, layer_weights, senders, receivers, live, flags):
    (
        edge_first,
        edge_bias,
        edge_second,
        edge_offset,
        edge_gain,
        node_first,
        node_bias,
        node_second,
        node_offset,
        node_gain,
        outlet_map,
    ) = layer_weights
    own = latent.astype(jnp.bfloat16)
    extended = jnp.concatenate([own, halo], axis=0)
    joined = jnp.concatenate(
        [edge_state.astype(jnp.bfloat16), extended[senders], own[receivers]], axis=1
    )
    act_one = jax.nn.silu(
        jnp.dot(joined, edge_first.astype(jnp.bfloat16), preferred_element_type=jnp.float32)
        + edge_bias
    ).astype(jnp.bfloat16)
    pre_two = (
        jnp.dot(act_one, edge_second.astype(jnp.bfloat16), preferred_element_type=jnp.float32)
        + edge_offset
    )
    message = live[:, None] * (edge_gain * normalize(pre_two))
    new_edge = edge_state + message
    summed = jax.ops.segment_sum(message, receivers, num_segments=latent.shape[0])
    summed_half = summed.astype(jnp.bfloat16)
    node_in = jnp.concatenate([own, summed_half], axis=1)
    node_hidden = jax.nn.silu(
        jnp.dot(node_in, node_first.astype(jnp.bfloat16), preferred_element_type=jnp.float32)
        + node_bias
    ).astype(jnp.bfloat16)
    update = node_gain * normalize(
        jnp.dot(node_hidden, node_second.astype(jnp.bfloat16), preferred_element_type=jnp.float32)
        + node_offset
    )
    outlet = flags[:, None] * jnp.dot(
        summed_half, outlet_map.astype(jnp.bfloat16), preferred_element_type=jnp.float32
    )
    return (latent + update + outlet, new_edge)


def send_halo(latent, send_rows, low, high):
    sent = latent[send_rows].astype(jnp.bfloat16)
    from_lower = passed_along(sent[low : 2 * low], "sub", 1)
    from_upper = passed_along(sent[:low], "sub", -1)
    dom_lower = passed_along(sent[2 * low + high :], "dom", 1)
    dom_upper = passed_along(sent[2 * low : 2 * low + high], "dom", -1)
    return jnp.concatenate([from_lower, from_upper, dom_lower, dom_upper], axis=0)


def return_halo(halo_grad, send_rows, low, high, shape):
    back_high = passed_along(halo_grad[:low], "sub", -1)
    back_low = passed_along(halo_grad[low : 2 * low], "sub", 1)
    dom_back_high = passed_along(halo_grad[2 * low : 2 * low + high], "dom", -1)
    dom_back_low = passed_along(halo_grad[2 * low + high :], "dom", 1)
    returned = jnp.concatenate([back_low, back_high, dom_back_low, dom_back_high], axis=0).astype(
        jnp.float32
    )
    return jnp.zeros(shape, jnp.float32).at[send_rows].add(returned)


def flatten_all(grads):
    return jnp.concatenate([grad.reshape(-1) for grad in grads])


def unflatten_all(flat, shapes):
    pieces = []
    offset = 0
    for shape in shapes:
        length = 1
        for extent in shape:
            length = length * extent
        pieces.append(flat[offset : offset + length].reshape(shape))
        offset = offset + length
    return pieces


def on_device(
    nodes,
    edges,
    senders,
    receivers,
    edge_live,
    outlet_flags,
    send_rows,
    edge_first,
    edge_bias,
    edge_second,
    edge_offset,
    edge_gain,
    node_first,
    node_bias,
    node_second,
    node_offset,
    node_gain,
    outlet_map,
    grad_out,
):
    weights = (
        edge_first,
        edge_bias,
        edge_second,
        edge_offset,
        edge_gain,
        node_first,
        node_bias,
        node_second,
        node_offset,
        node_gain,
        outlet_map,
    )
    layers = edge_first.shape[0]
    low = nodes.shape[0] // 8
    high = nodes.shape[0] // 4
    live = edge_live.astype(jnp.float32)
    flags = outlet_flags.astype(jnp.float32)
    latent = nodes.astype(jnp.float32)
    edge_state = edges.astype(jnp.float32)

    def advance(latent_in, edge_in, halo, layer_weights):
        return layer_local(latent_in, edge_in, halo, layer_weights, senders, receivers, live, flags)

    saved = []
    for layer in range(layers):
        layer_weights = tuple((weight[layer] for weight in weights))
        halo = send_halo(latent, send_rows, low, high)
        (latent, edge_state), pullback = jax.vjp(advance, latent, edge_state, halo, layer_weights)
        saved.append(pullback)
    layer_shapes = [weight.shape[1:] for weight in weights]
    latent_grad = grad_out
    edge_grad = jnp.zeros_like(edge_state)
    per_layer = [None] * layers
    for layer in reversed(range(layers)):
        pullback = saved[layer]
        latent_grad, edge_grad, halo_grad, weight_grads = pullback((latent_grad, edge_grad))
        latent_grad = latent_grad + return_halo(halo_grad, send_rows, low, high, latent_grad.shape)
        flat = flatten_all(weight_grads)
        per_layer[layer] = flat
    stacked = jnp.stack(per_layer, axis=0)
    stacked = lax.psum(stacked, ("dom", "sub"))
    by_layer = [unflatten_all(stacked[layer], layer_shapes) for layer in range(layers)]
    results = [
        jnp.stack([by_layer[layer][which] for layer in range(layers)], axis=0)
        for which in range(len(weights))
    ]
    return (
        latent,
        latent_grad,
        results[0],
        results[1],
        results[2],
        results[3],
        results[4],
        results[5],
        results[6],
        results[7],
        results[8],
        results[9],
        results[10],
    )


def solution(mesh):
    placed = (
        P(("dom", "sub"), None),
        P(("dom", "sub"), None),
        P(("dom", "sub")),
        P(("dom", "sub")),
        P(("dom", "sub")),
        P(("dom", "sub")),
        P(("dom", "sub")),
        P(),
        P(),
        P(),
        P(),
        P(),
        P(),
        P(),
        P(),
        P(),
        P(),
        P(),
        P(("dom", "sub"), None),
    )
    return jax.shard_map(
        on_device,
        mesh=mesh,
        in_specs=placed,
        out_specs=(
            P(("dom", "sub"), None),
            P(("dom", "sub"), None),
            P(),
            P(),
            P(),
            P(),
            P(),
            P(),
            P(),
            P(),
            P(),
            P(),
            P(),
        ),
        check_vma=False,
    )
```

profile of v0, /device:TPU:0, one launch (start us, length us, event | category | flops | bytes accessed | tf_op | source)
XLA Modules:
  0.0 548.7 jit_solution(7893833300528265434)
XLA Ops:
  12.7 3.8 collective-permute-start
  18.4 6.1 %collective-permute-start.2 = (bf16[128,128]{1,0:T(8,128)(2,1)}, bf16[128,128]{1,0:T(8,128)(2,1)}, u32[]{:S(2)}, u32[]{:S(2)}) collective-permute-start(bf16[128,128]{1,0:T(8,128)(2,1)} %get-tuple-element.114), channel_id=1, source_target_pairs={{0,4},{4,8},{8,12},{12,16},{16,20},{20,24},{24,28},{1,5},{5,9},{9,... | collective-permute-start | bytes 98312 | tf_op jit(solution)/shard_map/ppermute | solution.py:10
  33.6 6.2 %gather_fusion.2 = bf16[2048,128]{1,0:T(8,128)(2,1)S(1)} fusion(bf16[512,128]{1,0:T(8,128)(2,1)S(1)} %copy-done, s32[2048]{0:T(1024)S(1)} %get-tuple-element.118), kind=kCustom, calls=%fused_computation.2 | custom fusion | bytes 1056768 | tf_op jit(solution)/shard_map/jvp()/gather | solution.py:37
  42.0 6.2 %gather_fusion.1 = bf16[2048,128]{1,0:T(8,128)(2,1)S(1)} fusion(bf16[896,128]{1,0:T(8,128)(2,1)S(1)} %constant_dynamic-update-slice_fusion, s32[2048]{0:T(1024)S(1)} %get-tuple-element.121), kind=kCustom, calls=%fused_computation.1 | custom fusion | bytes 1056768 | tf_op jit(solution)/shard_map/jvp()/gather | solution.py:37
  53.7 11.9 %scatter_custom_fusion = f32[512,128]{1,0:T(8,128)S(1)} fusion(s32[2048]{0:T(1024)S(1)} %copy-done.84, f32[2048,128]{1,0:T(8,128)} %copy.74, f32[]{:T(128)} %constant.51.clone.1), kind=kCustom, calls=%fused_computation.256 | custom fusion | flops 262144 | bytes 262656 | tf_op jit(solution)/shard_map/jvp()/scatter-add | solution.py:49
  71.2 5.5 collective-permute-start.6
  82.0 6.2 %gather_fusion.5 = bf16[2048,128]{1,0:T(8,128)(2,1)S(1)} fusion(bf16[512,128]{1,0:T(8,128)(2,1)S(1)} %copy.80, s32[2048]{0:T(1024)S(1)} %copy-done.66), kind=kCustom, calls=%fused_computation.5 | custom fusion | bytes 1056768 | tf_op jit(solution)/shard_map/jvp()/gather | solution.py:37
  91.0 6.2 %gather_fusion.4 = bf16[2048,128]{1,0:T(8,128)(2,1)S(1)} fusion(bf16[896,128]{1,0:T(8,128)(2,1)S(1)} %copy.79, s32[2048]{0:T(1024)S(1)} %copy-done.60), kind=kCustom, calls=%fused_computation.4 | custom fusion | bytes 1056768 | tf_op jit(solution)/shard_map/jvp()/gather | solution.py:37
  106.6 11.9 %scatter_custom_fusion.1 = f32[512,128]{1,0:T(8,128)S(1)} fusion(s32[2048]{0:T(1024)S(1)} %copy-done.85, f32[2048,128]{1,0:T(8,128)} %copy.83, f32[]{:T(128)} %constant.51.clone.1), kind=kCustom, calls=%fused_computation.254 | custom fusion | flops 262144 | bytes 262656 | tf_op jit(solution)/shard_map/jvp()/scatter-add | solution.py:49
  126.5 4.4 collective-permute-start.8
  132.2 5.3 collective-permute-start.10
  137.7 7.2 %gather_fusion.8 = bf16[2048,128]{1,0:T(8,128)(2,1)S(1)} fusion(bf16[512,128]{1,0:T(8,128)(2,1)S(1)} %copy.89, s32[2048]{0:T(1024)} %copy-done.65), kind=kCustom, calls=%fused_computation.8 | custom fusion | bytes 1056768 | tf_op jit(solution)/shard_map/jvp()/gather | solution.py:37
  147.1 7.2 %gather_fusion.7 = bf16[2048,128]{1,0:T(8,128)(2,1)S(1)} fusion(bf16[896,128]{1,0:T(8,128)(2,1)S(1)} %copy.88, s32[2048]{0:T(1024)} %copy-done.59), kind=kCustom, calls=%fused_computation.7 | custom fusion | bytes 1056768 | tf_op jit(solution)/shard_map/jvp()/gather | solution.py:37
  163.6 12.9 %scatter_custom_fusion.2 = f32[512,128]{1,0:T(8,128)} fusion(s32[2048]{0:T(1024)} %param.22, f32[2048,128]{1,0:T(8,128)} %copy.92, f32[]{:T(128)} %constant.51.clone.1), kind=kCustom, calls=%fused_computation.252 | custom fusion | flops 262144 | bytes 262656 | tf_op jit(solution)/shard_map/jvp()/scatter-add | solution.py:49
  190.0 8.4 %gather_fusion.9 = f32[2048,128]{1,0:T(8,128)} fusion(f32[512,128]{1,0:T(8,128)S(1)} %fusion.19, s32[2048]{0:T(1024)} %get-tuple-element.119), kind=kCustom, calls=%fused_computation.9 | custom fusion | bytes 2105344 | tf_op jit(solution)/shard_map/transpose(jvp())/gather | solution.py:49
  212.5 11.9 %scatter_custom_fusion.3 = bf16[896,128]{1,0:T(8,128)(2,1)S(1)} fusion(s32[2048]{0:T(1024)} %get-tuple-element.120, bf16[2048,128]{1,0:T(8,128)(2,1)} %copy.99, bf16[]{:T(256)} %constant.59.clone.1), kind=kCustom, calls=%fused_computation.261 | custom fusion | flops 262144 | bytes 229888 | tf_op jit(solution)/shard_map/transpose(jvp())/scatter-add | solution.py:37
  226.9 3.4 collective-permute-start.12
  231.6 4.6 collective-permute-start.14
  237.4 11.9 %scatter_fusion = bf16[512,128]{1,0:T(8,128)(2,1)S(1)} fusion(bf16[512,128]{1,0:T(8,128)(2,1)S(1)} %slice_add_fusion.2, s32[2048]{0:T(1024)} %get-tuple-element.117, bf16[2048,128]{1,0:T(8,128)(2,1)S(1)} %copy.100), kind=kCustom, calls=%fused_computation.16 | custom fusion | flops 262144 | bytes 1581056 | tf_op jit(solution)/shard_map/transpose(jvp())/scatter-add | solution.py:37
  264.3 3.6 stack.26
  279.9 7.6 %gather_fusion.10 = f32[2048,128]{1,0:T(8,128)} fusion(f32[512,128]{1,0:T(8,128)S(1)} %fusion.21, s32[2048]{0:T(1024)S(1)} %copy-done.70), kind=kCustom, calls=%fused_computation.10 | custom fusion | bytes 2105344 | tf_op jit(solution)/shard_map/transpose(jvp())/gather | solution.py:49
  301.4 11.9 %scatter_custom_fusion.6 = bf16[896,128]{1,0:T(8,128)(2,1)S(1)} fusion(s32[2048]{0:T(1024)} %get-tuple-element.120, bf16[2048,128]{1,0:T(8,128)(2,1)} %copy.105, bf16[]{:T(256)} %constant.59.clone.1), kind=kCustom, calls=%fused_computation.259 | custom fusion | flops 262144 | bytes 229888 | tf_op jit(solution)/shard_map/transpose(jvp())/scatter-add | solution.py:37
  315.9 11.8 %scatter_fusion.1 = bf16[512,128]{1,0:T(8,128)(2,1)S(1)} fusion(bf16[512,128]{1,0:T(8,128)(2,1)S(1)} %slice_add_fusion.1, s32[2048]{0:T(1024)} %get-tuple-element.117, bf16[2048,128]{1,0:T(8,128)(2,1)S(1)} %copy.106), kind=kCustom, calls=%fused_computation.19 | custom fusion | flops 262144 | bytes 1581056 | tf_op jit(solution)/shard_map/transpose(jvp())/scatter-add | solution.py:37
  332.8 4.3 collective-permute-start.18
  352.6 3.6 stack.25
  368.5 8.4 %gather_fusion.11 = f32[2048,128]{1,0:T(8,128)} fusion(f32[512,128]{1,0:T(8,128)S(1)} %fusion.23, s32[2048]{0:T(1024)} %get-tuple-element.119), kind=kCustom, calls=%fused_computation.11 | custom fusion | bytes 2105344 | tf_op jit(solution)/shard_map/transpose(jvp())/gather | solution.py:49
  392.2 11.9 %scatter_custom_fusion.9 = bf16[896,128]{1,0:T(8,128)(2,1)S(1)} fusion(s32[2048]{0:T(1024)} %get-tuple-element.120, bf16[2048,384]{1,0:T(8,128)(2,1)S(1)} %convolution_convert_fusion, bf16[]{:T(256)} %constant.59.clone.1), kind=kCustom, calls=%fused_computation.171 | custom fusion | flops 262144 | bytes 754176 | tf_op jit(solution)/shard_map/transpose(jvp())/scatter-add | solution.py:37
  404.1 12.0 %scatter_custom_fusion.10 = bf16[512,128]{1,0:T(8,128)(2,1)S(1)} fusion(bf16[512,128]{1,0:T(8,128)(2,1)S(1)} %slice_add_fusion, s32[2048]{0:T(1024)} %get-tuple-element.117, bf16[2048,384]{1,0:T(8,128)(2,1)S(1)} %convolution_convert_fusion), kind=kCustom, calls=%fused_computation.169 | custom fusion | flops 262144 | bytes 655360 | tf_op jit(solution)/shard_map/transpose(jvp())/scatter-add | solution.py:37
  416.1 4.0 collective-permute-start.20
  421.4 4.3 collective-permute-start.22
  427.3 4.2 collective-permute-done.23
  434.4 96.1 %all-reduce.2.cloned.1.call-done = f32[3,131840]{1,0:T(4,128)} async-done(((f32[3,131840]{1,0:T(4,128)}), f32[3,131840]{1,0:T(4,128)}) %all-reduce.2.cloned.1.call-update) | async-done | bytes 1582096 | tf_op jit(solution)/shard_map/psum | solution.py:164
  (523 shorter events, 207.2 us)
Async XLA Ops:
  7.3 523.3 %all-reduce.2.cloned.1.call-start = ((), (), s32[]{:S(2)}) async-start(), calls=%async_computation | async-start | bytes 4218880 | tf_op jit(solution)/shard_map/psum | solution.py:164
  11.4 29.1 %collective-permute-start.1 = (bf16[64,128]{1,0:T(8,128)(2,1)}, bf16[64,128]{1,0:T(8,128)(2,1)}, u32[]{:S(2)}, u32[]{:S(2)}) collective-permute-start(bf16[64,128]{1,0:T(8,128)(2,1)} %get-tuple-element.115), channel_id=1, source_target_pairs={{1,0},{2,1},{3,2},{5,4},{6,5},{7,6},{9,8},{10,9},{11,10},{13,12},{... | collective-permute-start | bytes 49160 | tf_op jit(solution)/shard_map/ppermute | solution.py:10
  12.7 27.1 %collective-permute-start = (bf16[64,128]{1,0:T(8,128)(2,1)}, bf16[64,128]{1,0:T(8,128)(2,1)}, u32[]{:S(2)}, u32[]{:S(2)}) collective-permute-start(bf16[64,128]{1,0:T(8,128)(2,1)} %get-tuple-element.116), channel_id=1, source_target_pairs={{0,1},{1,2},{2,3},{4,5},{5,6},{6,7},{8,9},{9,10},{10,11},{12,13},{... | collective-permute-start | bytes 49160 | tf_op jit(solution)/shard_map/ppermute | solution.py:10
  17.1 24.9 %collective-permute-start.3 = (bf16[128,128]{1,0:T(8,128)(2,1)}, bf16[128,128]{1,0:T(8,128)(2,1)S(1)}, u32[]{:S(2)}, u32[]{:S(2)}) collective-permute-start(bf16[128,128]{1,0:T(8,128)(2,1)} %get-tuple-element.113), channel_id=1, source_target_pairs={{4,0},{8,4},{12,8},{16,12},{20,16},{24,20},{28,24},{5,1},{9,5},{13... | collective-permute-start | bytes 98312 | tf_op jit(solution)/shard_map/ppermute | solution.py:10
  18.4 22.8 %collective-permute-start.2 = (bf16[128,128]{1,0:T(8,128)(2,1)}, bf16[128,128]{1,0:T(8,128)(2,1)}, u32[]{:S(2)}, u32[]{:S(2)}) collective-permute-start(bf16[128,128]{1,0:T(8,128)(2,1)} %get-tuple-element.114), channel_id=1, source_target_pairs={{0,4},{4,8},{8,12},{12,16},{16,20},{20,24},{24,28},{1,5},{5,9},{9,... | collective-permute-start | bytes 98312 | tf_op jit(solution)/shard_map/ppermute | solution.py:10
  32.3 33.3 %copy-start.41 = (bf16[3,256,128]{2,1,0:T(8,128)(2,1)}, bf16[3,256,128]{2,1,0:T(8,128)(2,1)S(1)}, u32[]{:S(2)}) copy-start(bf16[3,256,128]{2,1,0:T(8,128)(2,1)S(1)} %convert.42) | copy-start | bytes 589828
  69.9 19.4 %collective-permute-start.7 = (bf16[128,128]{0,1:T(8,128)(2,1)S(1)}, bf16[128,128]{0,1:T(8,128)(2,1)}, u32[]{:S(2)}, u32[]{:S(2)}) collective-permute-start(bf16[128,128]{0,1:T(8,128)(2,1)S(1)} %get-tuple-element.109), channel_id=1, source_target_pairs={{4,0},{8,4},{12,8},{16,12},{20,16},{24,20},{28,24},{5,1},{9,5},{13... | collective-permute-start | bytes 98312 | tf_op jit(solution)/shard_map/ppermute | solution.py:10
  71.2 18.7 %collective-permute-start.6 = (bf16[128,128]{0,1:T(8,128)(2,1)S(1)}, bf16[128,128]{0,1:T(8,128)(2,1)}, u32[]{:S(2)}, u32[]{:S(2)}) collective-permute-start(bf16[128,128]{0,1:T(8,128)(2,1)S(1)} %get-tuple-element.110), channel_id=1, source_target_pairs={{0,4},{4,8},{8,12},{12,16},{16,20},{20,24},{24,28},{1,5},{5,9},{9,... | collective-permute-start | bytes 98312 | tf_op jit(solution)/shard_map/ppermute | solution.py:10
  77.3 12.0 %collective-permute-start.5 = (bf16[64,128]{0,1:T(8,128)(2,1)}, bf16[64,128]{0,1:T(8,128)(2,1)S(1)}, u32[]{:S(2)}, u32[]{:S(2)}) collective-permute-start(bf16[64,128]{0,1:T(8,128)(2,1)} %get-tuple-element.111), channel_id=1, source_target_pairs={{1,0},{2,1},{3,2},{5,4},{6,5},{7,6},{9,8},{10,9},{11,10},{13,12},{... | collective-permute-start | bytes 49160 | tf_op jit(solution)/shard_map/ppermute | solution.py:10
  78.6 10.7 %collective-permute-start.4 = (bf16[64,128]{0,1:T(8,128)(2,1)S(1)}, bf16[64,128]{0,1:T(8,128)(2,1)S(1)}, u32[]{:S(2)}, u32[]{:S(2)}) collective-permute-start(bf16[64,128]{0,1:T(8,128)(2,1)S(1)} %get-tuple-element.112), channel_id=1, source_target_pairs={{0,1},{1,2},{2,3},{4,5},{5,6},{6,7},{8,9},{9,10},{10,11},{12,13},{... | collective-permute-start | bytes 49160 | tf_op jit(solution)/shard_map/ppermute | solution.py:10
  122.1 22.8 %copy-start.13 = (f32[512,128]{0,1:T(8,128)}, f32[512,128]{0,1:T(8,128)S(1)}, u32[]{:S(2)}) copy-start(f32[512,128]{0,1:T(8,128)S(1)} %get-tuple-element.151) | copy-start | bytes 786436
  122.1 23.8 %copy-start.30 = (bf16[512,128]{0,1:T(8,128)(2,1)}, bf16[512,128]{0,1:T(8,128)(2,1)S(1)}, u32[]{:S(2)}) copy-start(bf16[512,128]{0,1:T(8,128)(2,1)S(1)} %get-tuple-element.150) | copy-start | bytes 393220
  125.2 20.8 %collective-permute-start.9 = (bf16[64,128]{0,1:T(8,128)(2,1)}, bf16[64,128]{0,1:T(8,128)(2,1)}, u32[]{:S(2)}, u32[]{:S(2)}) collective-permute-start(bf16[64,128]{0,1:T(8,128)(2,1)} %get-tuple-element.107), channel_id=1, source_target_pairs={{1,0},{2,1},{3,2},{5,4},{6,5},{7,6},{9,8},{10,9},{11,10},{13,12},{... | collective-permute-start | bytes 49160 | tf_op jit(solution)/shard_map/ppermute | solution.py:10
  126.5 19.5 %collective-permute-start.8 = (bf16[64,128]{0,1:T(8,128)(2,1)}, bf16[64,128]{0,1:T(8,128)(2,1)}, u32[]{:S(2)}, u32[]{:S(2)}) collective-permute-start(bf16[64,128]{0,1:T(8,128)(2,1)} %get-tuple-element.108), channel_id=1, source_target_pairs={{0,1},{1,2},{2,3},{4,5},{5,6},{6,7},{8,9},{9,10},{10,11},{12,13},{... | collective-permute-start | bytes 49160 | tf_op jit(solution)/shard_map/ppermute | solution.py:10
  130.9 15.1 %collective-permute-start.11 = (bf16[128,128]{0,1:T(8,128)(2,1)}, bf16[128,128]{0,1:T(8,128)(2,1)}, u32[]{:S(2)}, u32[]{:S(2)}) collective-permute-start(bf16[128,128]{0,1:T(8,128)(2,1)} %get-tuple-element.105), channel_id=1, source_target_pairs={{4,0},{8,4},{12,8},{16,12},{20,16},{24,20},{28,24},{5,1},{9,5},{13... | collective-permute-start | bytes 98312 | tf_op jit(solution)/shard_map/ppermute | solution.py:10
  132.2 13.8 %collective-permute-start.10 = (bf16[128,128]{0,1:T(8,128)(2,1)}, bf16[128,128]{0,1:T(8,128)(2,1)}, u32[]{:S(2)}, u32[]{:S(2)}) collective-permute-start(bf16[128,128]{0,1:T(8,128)(2,1)} %get-tuple-element.106), channel_id=1, source_target_pairs={{0,4},{4,8},{8,12},{12,16},{16,20},{20,24},{24,28},{1,5},{5,9},{9,... | collective-permute-start | bytes 98312 | tf_op jit(solution)/shard_map/ppermute | solution.py:10
  137.6 46.4 %copy-start.5 = (f32[512,128]{0,1:T(8,128)}, f32[512,128]{0,1:T(8,128)S(1)}, u32[]{:S(2)}) copy-start(f32[512,128]{0,1:T(8,128)S(1)} %copy.95) | copy-start | bytes 786436
  226.9 41.0 %collective-permute-start.12 = (bf16[64,128]{1,0:T(8,128)(2,1)}, bf16[64,128]{1,0:T(8,128)(2,1)}, u32[]{:S(2)}, u32[]{:S(2)}) collective-permute-start(bf16[64,128]{1,0:T(8,128)(2,1)} %get-tuple-element.101), channel_id=1, source_target_pairs={{0,1},{1,2},{2,3},{4,5},{5,6},{6,7},{8,9},{9,10},{10,11},{12,13},{... | collective-permute-start | bytes 49160 | tf_op jit(solution)/shard_map/ppermute | solution.py:10
  230.3 37.6 %collective-permute-start.13 = (bf16[64,128]{1,0:T(8,128)(2,1)}, bf16[64,128]{1,0:T(8,128)(2,1)}, u32[]{:S(2)}, u32[]{:S(2)}) collective-permute-start(bf16[64,128]{1,0:T(8,128)(2,1)} %get-tuple-element.102), channel_id=1, source_target_pairs={{1,0},{2,1},{3,2},{5,4},{6,5},{7,6},{9,8},{10,9},{11,10},{13,12},{... | collective-permute-start | bytes 49160 | tf_op jit(solution)/shard_map/ppermute | solution.py:10
  231.6 36.3 %collective-permute-start.14 = (bf16[128,128]{1,0:T(8,128)(2,1)}, bf16[128,128]{1,0:T(8,128)(2,1)}, u32[]{:S(2)}, u32[]{:S(2)}) collective-permute-start(bf16[128,128]{1,0:T(8,128)(2,1)} %get-tuple-element.103), channel_id=1, source_target_pairs={{0,4},{4,8},{8,12},{12,16},{16,20},{20,24},{24,28},{1,5},{5,9},{9,... | collective-permute-start | bytes 98312 | tf_op jit(solution)/shard_map/ppermute | solution.py:10
  236.1 31.8 %collective-permute-start.15 = (bf16[128,128]{1,0:T(8,128)(2,1)}, bf16[128,128]{1,0:T(8,128)(2,1)}, u32[]{:S(2)}, u32[]{:S(2)}) collective-permute-start(bf16[128,128]{1,0:T(8,128)(2,1)} %get-tuple-element.104), channel_id=1, source_target_pairs={{4,0},{8,4},{12,8},{16,12},{20,16},{24,20},{28,24},{5,1},{9,5},{13... | collective-permute-start | bytes 98312 | tf_op jit(solution)/shard_map/ppermute | solution.py:10
  237.4 26.1 %copy-start.32 = (f32[512,128]{0,1:T(8,128)S(1)}, f32[512,128]{0,1:T(8,128)}, u32[]{:S(2)}) copy-start(f32[512,128]{0,1:T(8,128)} %fusion.3) | copy-start | bytes 786436
  327.7 31.5 %copy-start.10 = (f32[512,128]{0,1:T(8,128)S(1)}, f32[512,128]{0,1:T(8,128)}, u32[]{:S(2)}) copy-start(f32[512,128]{0,1:T(8,128)} %copy-done.9) | copy-start | bytes 786436
  328.7 27.4 %collective-permute-start.16 = (bf16[64,128]{1,0:T(8,128)(2,1)}, bf16[64,128]{1,0:T(8,128)(2,1)S(1)}, u32[]{:S(2)}, u32[]{:S(2)}) collective-permute-start(bf16[64,128]{1,0:T(8,128)(2,1)} %get-tuple-element.97), channel_id=1, source_target_pairs={{0,1},{1,2},{2,3},{4,5},{5,6},{6,7},{8,9},{9,10},{10,11},{12,13},{... | collective-permute-start | bytes 49160 | tf_op jit(solution)/shard_map/ppermute | solution.py:10
  331.5 24.7 %collective-permute-start.17 = (bf16[64,128]{1,0:T(8,128)(2,1)}, bf16[64,128]{1,0:T(8,128)(2,1)S(1)}, u32[]{:S(2)}, u32[]{:S(2)}) collective-permute-start(bf16[64,128]{1,0:T(8,128)(2,1)} %get-tuple-element.98), channel_id=1, source_target_pairs={{1,0},{2,1},{3,2},{5,4},{6,5},{7,6},{9,8},{10,9},{11,10},{13,12},{... | collective-permute-start | bytes 49160 | tf_op jit(solution)/shard_map/ppermute | solution.py:10
  332.8 23.4 %collective-permute-start.18 = (bf16[128,128]{1,0:T(8,128)(2,1)}, bf16[128,128]{1,0:T(8,128)(2,1)S(1)}, u32[]{:S(2)}, u32[]{:S(2)}) collective-permute-start(bf16[128,128]{1,0:T(8,128)(2,1)} %get-tuple-element.99), channel_id=1, source_target_pairs={{0,4},{4,8},{8,12},{12,16},{16,20},{20,24},{24,28},{1,5},{5,9},{9,... | collective-permute-start | bytes 98312 | tf_op jit(solution)/shard_map/ppermute | solution.py:10
  337.1 19.1 %collective-permute-start.19 = (bf16[128,128]{1,0:T(8,128)(2,1)}, bf16[128,128]{1,0:T(8,128)(2,1)S(1)}, u32[]{:S(2)}, u32[]{:S(2)}) collective-permute-start(bf16[128,128]{1,0:T(8,128)(2,1)} %get-tuple-element.100), channel_id=1, source_target_pairs={{4,0},{8,4},{12,8},{16,12},{20,16},{24,20},{28,24},{5,1},{9,5},{13... | collective-permute-start | bytes 98312 | tf_op jit(solution)/shard_map/ppermute | solution.py:10
  416.1 11.0 %collective-permute-start.20 = (bf16[64,128]{1,0:T(8,128)(2,1)S(1)}, bf16[64,128]{1,0:T(8,128)(2,1)S(1)}, u32[]{:S(2)}, u32[]{:S(2)}) collective-permute-start(bf16[64,128]{1,0:T(8,128)(2,1)S(1)} %get-tuple-element.93), channel_id=1, source_target_pairs={{0,1},{1,2},{2,3},{4,5},{5,6},{6,7},{8,9},{9,10},{10,11},{12,13},{... | collective-permute-start | bytes 49160 | tf_op jit(solution)/shard_map/ppermute | solution.py:10
  420.1 6.9 %collective-permute-start.21 = (bf16[64,128]{1,0:T(8,128)(2,1)S(1)}, bf16[64,128]{1,0:T(8,128)(2,1)S(1)}, u32[]{:S(2)}, u32[]{:S(2)}) collective-permute-start(bf16[64,128]{1,0:T(8,128)(2,1)S(1)} %get-tuple-element.94), channel_id=1, source_target_pairs={{1,0},{2,1},{3,2},{5,4},{6,5},{7,6},{9,8},{10,9},{11,10},{13,12},{... | collective-permute-start | bytes 49160 | tf_op jit(solution)/shard_map/ppermute | solution.py:10
  421.4 5.9 %collective-permute-start.22 = (bf16[128,128]{1,0:T(8,128)(2,1)S(1)}, bf16[128,128]{1,0:T(8,128)(2,1)S(1)}, u32[]{:S(2)}, u32[]{:S(2)}) collective-permute-start(bf16[128,128]{1,0:T(8,128)(2,1)S(1)} %get-tuple-element.95), channel_id=1, source_target_pairs={{0,4},{4,8},{8,12},{12,16},{16,20},{20,24},{24,28},{1,5},{5,9},{9,... | collective-permute-start | bytes 98312 | tf_op jit(solution)/shard_map/ppermute | solution.py:10
  425.7 5.8 %collective-permute-start.23 = (bf16[128,128]{1,0:T(8,128)(2,1)S(1)}, bf16[128,128]{1,0:T(8,128)(2,1)S(1)}, u32[]{:S(2)}, u32[]{:S(2)}) collective-permute-start(bf16[128,128]{1,0:T(8,128)(2,1)S(1)} %get-tuple-element.96), channel_id=1, source_target_pairs={{4,0},{8,4},{12,8},{16,12},{20,16},{24,20},{28,24},{5,1},{9,5},{13... | collective-permute-start | bytes 98312 | tf_op jit(solution)/shard_map/ppermute | solution.py:10
  434.4 101.7 %copy-start.49 = (f32[512,128]{1,0:T(8,128)}, f32[512,128]{1,0:T(8,128)S(1)}, u32[]{:S(2)}) copy-start(f32[512,128]{1,0:T(8,128)S(1)} %scatter_custom_fusion.11) | copy-start | bytes 786436
  (124 other events, 927.9 us)
Sparse Core Ops, SparseCore 0:
  392.3 138.2 all-reduce.1
where the time goes:
time: 559 us; the launch traced here: 549 us
  local copies, waits for them, and re-layouts  161 us (29%)
  other arithmetic  151 us (27%)
  waiting for transfers between devices  101 us (18%)
  starting transfers between devices  67.2 us (12%)
  matrix products  52.3 us (9%)
  between operations  16.9 us (3%)
    psum x1, waiting for transfers between devices, on_device(): stacked = lax.psum(stacked, ('dom', 'sub'))  96.1 us
    ppermute x24, starting transfers between devices, passed_along(): lax.ppermute(value, axis, [(source, source + steps) for source in range(f...  67.2 us
    scatter-add x3, other arithmetic, layer_local(): jax.ops.segment_sum(message, receivers, num_segments=latent.shape[0])  36.7 us
    unnamed x299, local copies, waits for them, and re-layouts  36.6 us
    scatter-add x3, other arithmetic, layer_local(): extended[senders]  35.8 us
    scatter-add x3, other arithmetic, layer_local(): own[receivers]  35.6 us
    gather x6, local copies, waits for them, and re-layouts, layer_local(): jax.ops.segment_sum(message, receivers, num_segments=latent.shape[0])  31 us
    gather x5, local copies, waits for them, and re-layouts, layer_local(): extended[senders]  21.6 us
  transfers between devices with their start and end apart: 25, of which 3 were waited for; matrix products, arithmetic and copies ran while one was open for 20% of the time, Pallas kernels for 0%

commit v1 on v0

--- a/solution.py
+++ b/solution.py
@@ -161,7 +161,7 @@
         flat = flatten_all(weight_grads)
         per_layer[layer] = flat
     stacked = jnp.stack(per_layer, axis=0)
-    stacked = lax.psum(stacked, ("dom", "sub"))
+    stacked = jnp.sum(lax.all_gather(stacked, ("dom", "sub")), axis=0)
     by_layer = [unflatten_all(stacked[layer], layer_shapes) for layer in range(layers)]
     results = [
         jnp.stack([by_layer[layer][which] for layer in range(layers)], axis=0)

time: 559 us -> 803 us (1.44)
  waiting for transfers between devices: 101 us -> 316 us
  other arithmetic: 151 us -> 174 us
    all_gather x0 -> x1, waiting for transfers between devices: none -> 316 us  [on_device(): stacked = jnp.sum(lax.all_gather(stacked, ('dom', 'sub')), axis=0)]
    psum x1 -> x0, waiting for transfers between devices: 96.1 us -> none  [on_device(): stacked = lax.psum(stacked, ('dom', 'sub'))]
    reduce_sum x0 -> x1, other arithmetic: none -> 21.7 us  [on_device(): stacked = jnp.sum(lax.all_gather(stacked, ('dom', 'sub')), axis=0)]
    unnamed x299 -> x377, local copies, waits for them, and re-layouts: 36.6 us -> 39.5 us
  transfers between devices with their start and end apart: 25 -> 25, of which waited for: 3 -> 1; matrix products, arithmetic and copies ran while one was open for 20% -> 13% of each run, Pallas kernels for 0% -> 0%
where the time goes in v1:
time: 803 us; the launch traced here: 792 us
  waiting for transfers between devices  316 us (39%)
  other arithmetic  174 us (22%)
  local copies, waits for them, and re-layouts  162 us (20%)
  starting transfers between devices  71 us (9%)
  matrix products  52.4 us (7%)
  between operations  17.3 us (2%)
    all_gather x1, waiting for transfers between devices, on_device(): stacked = jnp.sum(lax.all_gather(stacked, ('dom', 'sub')), axis=0)  316 us
    ppermute x24, starting transfers between devices, passed_along(): lax.ppermute(value, axis, [(source, source + steps) for source in range(f...  70.9 us
    unnamed x377, local copies, waits for them, and re-layouts  39.5 us
    scatter-add x3, other arithmetic, layer_local(): jax.ops.segment_sum(message, receivers, num_segments=latent.shape[0])  36.7 us
    scatter-add x3, other arithmetic, layer_local(): extended[senders]  35.6 us
    scatter-add x3, other arithmetic, layer_local(): own[receivers]  35.6 us
    gather x6, local copies, waits for them, and re-layouts, layer_local(): jax.ops.segment_sum(message, receivers, num_segments=latent.shape[0])  31.6 us
    gather x5, local copies, waits for them, and re-layouts, layer_local(): extended[senders]  22.5 us
  transfers between devices with their start and end apart: 25, of which 1 were waited for; matrix products, arithmetic and copies ran while one was open for 13% of the time, Pallas kernels for 0%

profile of v1, /device:TPU:0, one launch (start us, length us, event | category | flops | bytes accessed | tf_op | source)
XLA Modules:
  0.0 792.1 jit_solution(8090417507786891548)
XLA Ops:
  16.9 4.8 collective-permute-start.2
  29.4 6.2 gather_fusion.2
  42.5 7.2 gather_fusion.1
  55.1 11.9 %scatter_custom_fusion = f32[512,128]{1,0:T(8,128)S(1)} fusion(s32[2048]{0:T(1024)} %param.22, f32[2048,128]{1,0:T(8,128)} %copy.116, f32[]{:T(128)} %constant.51.clone.1), kind=kCustom, calls=%fused_computation.256 | custom fusion | flops 262144 | bytes 262656 | tf_op jit(solution)/shard_map/jvp()/scatter-add | solution.py:49
  71.3 5.2 collective-permute-start.6
  83.0 6.2 gather_fusion.5
  91.9 6.2 gather_fusion.4
  107.5 11.9 %scatter_custom_fusion.1 = f32[512,128]{1,0:T(8,128)S(1)} fusion(s32[2048]{0:T(1024)S(1)} %copy-done.109, f32[2048,128]{1,0:T(8,128)} %copy.125, f32[]{:T(128)} %constant.51.clone.1), kind=kCustom, calls=%fused_computation.254 | custom fusion | flops 262144 | bytes 262656 | tf_op jit(solution)/shard_map/jvp()/scatter-add | solution.py:49
  126.1 5.7 collective-permute-start.8
  133.1 5.2 collective-permute-start.10
  139.8 7.2 gather_fusion.8
  149.1 7.2 gather_fusion.7
  165.8 12.9 %scatter_custom_fusion.2 = f32[512,128]{1,0:T(8,128)} fusion(s32[2048]{0:T(1024)} %param.22, f32[2048,128]{1,0:T(8,128)} %copy.134, f32[]{:T(128)} %constant.51.clone.1), kind=kCustom, calls=%fused_computation.252 | custom fusion | flops 262144 | bytes 262656 | tf_op jit(solution)/shard_map/jvp()/scatter-add | solution.py:49
  188.7 8.3 %gather_fusion.9 = f32[2048,128]{1,0:T(8,128)} fusion(f32[512,128]{1,0:T(8,128)S(1)} %fusion.19, s32[2048]{0:T(1024)} %get-tuple-element.132), kind=kCustom, calls=%fused_computation.9 | custom fusion | bytes 2105344 | tf_op jit(solution)/shard_map/transpose(jvp())/gather | solution.py:49
  208.8 11.9 %scatter_custom_fusion.3 = bf16[896,128]{1,0:T(8,128)(2,1)S(1)} fusion(s32[2048]{0:T(1024)} %get-tuple-element.133, bf16[2048,128]{1,0:T(8,128)(2,1)} %copy.141, bf16[]{:T(256)} %constant.59.clone.1), kind=kCustom, calls=%fused_computation.261 | custom fusion | flops 262144 | bytes 229888 | tf_op jit(solution)/shard_map/transpose(jvp())/scatter-add | solution.py:37
  230.9 11.6 %scatter_fusion = bf16[512,128]{1,0:T(8,128)(2,1)S(1)} fusion(bf16[512,128]{1,0:T(8,128)(2,1)S(1)} %slice_add_fusion.2, s32[2048]{0:T(1024)S(1)} %copy-done.83, bf16[2048,128]{1,0:T(8,128)(2,1)S(1)} %copy.142), kind=kCustom, calls=%fused_computation.16 | custom fusion | flops 262144 | bytes 1581056 | tf_op jit(solution)/shard_map/transpose(jvp())/scatter-add | solution.py:37
  244.1 5.2 collective-permute-start.14
  268.0 3.6 stack.26
  279.7 8.3 %gather_fusion.10 = f32[2048,128]{1,0:T(8,128)} fusion(f32[512,128]{1,0:T(8,128)S(1)} %fusion.21, s32[2048]{0:T(1024)} %get-tuple-element.132), kind=kCustom, calls=%fused_computation.10 | custom fusion | bytes 2105344 | tf_op jit(solution)/shard_map/transpose(jvp())/gather | solution.py:49
  298.7 11.9 %scatter_custom_fusion.6 = bf16[896,128]{1,0:T(8,128)(2,1)S(1)} fusion(s32[2048]{0:T(1024)} %get-tuple-element.133, bf16[2048,128]{1,0:T(8,128)(2,1)} %copy.147, bf16[]{:T(256)} %constant.59.clone.1), kind=kCustom, calls=%fused_computation.259 | custom fusion | flops 262144 | bytes 229888 | tf_op jit(solution)/shard_map/transpose(jvp())/scatter-add | solution.py:37
  321.8 12.0 %scatter_fusion.1 = bf16[512,128]{1,0:T(8,128)(2,1)S(1)} fusion(bf16[512,128]{1,0:T(8,128)(2,1)S(1)} %slice_add_fusion.1, s32[2048]{0:T(1024)S(1)} %copy-done.84, bf16[2048,128]{1,0:T(8,128)(2,1)} %copy.148), kind=kCustom, calls=%fused_computation.19 | custom fusion | flops 262144 | bytes 1581056 | tf_op jit(solution)/shard_map/transpose(jvp())/scatter-add | solution.py:37
  335.9 5.2 collective-permute-start.18
  342.4 5.3 collective-permute-start.16
  361.8 3.6 stack.25
  365.4 4.2 scatter_custom_fusion.8
  375.5 8.3 %gather_fusion.11 = f32[2048,128]{1,0:T(8,128)} fusion(f32[512,128]{1,0:T(8,128)S(1)} %fusion.23, s32[2048]{0:T(1024)} %get-tuple-element.132), kind=kCustom, calls=%fused_computation.11 | custom fusion | bytes 2105344 | tf_op jit(solution)/shard_map/transpose(jvp())/gather | solution.py:49
  403.1 11.7 %scatter_custom_fusion.9 = bf16[896,128]{1,0:T(8,128)(2,1)S(1)} fusion(s32[2048]{0:T(1024)} %get-tuple-element.133, bf16[2048,384]{1,0:T(8,128)(2,1)S(1)} %convolution_convert_fusion, bf16[]{:T(256)} %constant.59.clone.1), kind=kCustom, calls=%fused_computation.171 | custom fusion | flops 262144 | bytes 754176 | tf_op jit(solution)/shard_map/transpose(jvp())/scatter-add | solution.py:37
  414.9 12.0 %scatter_custom_fusion.10 = bf16[512,128]{1,0:T(8,128)(2,1)S(1)} fusion(bf16[512,128]{1,0:T(8,128)(2,1)S(1)} %slice_add_fusion, s32[2048]{0:T(1024)} %get-tuple-element.130, bf16[2048,384]{1,0:T(8,128)(2,1)S(1)} %convolution_convert_fusion), kind=kCustom, calls=%fused_computation.169 | custom fusion | flops 262144 | bytes 655360 | tf_op jit(solution)/shard_map/transpose(jvp())/scatter-add | solution.py:37
  428.2 5.2 collective-permute-start.22
  434.7 4.0 collective-permute-start.20
  442.6 315.8 %all-gather.4.cloned.1.call-done = f32[32,3,131840]{2,1,0:T(4,128)} async-done(((f32[1,3,131840]{2,1,0:T(4,128)}), f32[32,3,131840]{2,1,0:T(4,128)}) %all-gather.4.cloned.1.call-update) | async-done | bytes 50626576 | tf_op jit(solution)/shard_map/all_gather | solution.py:164
  758.4 21.7 %reduce_sum.449 = f32[3,131840]{1,0:T(4,128)S(1)} reduce(f32[32,3,131840]{2,1,0:T(4,128)} %all-gather.4.cloned.1.call-done, f32[]{:T(128)} %constant.51.clone.1), dimensions={0}, to_apply=%region_54.55 | reduce | flops 12261120 | bytes 52208644 | tf_op jit(solution)/shard_map/reduce_sum | solution.py:164
  (602 shorter events, 207.6 us)
Async XLA Ops:
  7.3 751.1 %all-gather.4.cloned.1.call-start = ((), (), s32[]{:S(2)}) async-start(), calls=%async_computation | async-start | bytes 69611520 | tf_op jit(solution)/shard_map/all_gather | solution.py:164
  12.0 27.5 %collective-permute-start = (bf16[64,128]{1,0:T(8,128)(2,1)}, bf16[64,128]{1,0:T(8,128)(2,1)}, u32[]{:S(2)}, u32[]{:S(2)}) collective-permute-start(bf16[64,128]{1,0:T(8,128)(2,1)} %get-tuple-element.129), channel_id=1, source_target_pairs={{0,1},{1,2},{2,3},{4,5},{5,6},{6,7},{8,9},{9,10},{10,11},{12,13},{... | collective-permute-start | bytes 49160 | tf_op jit(solution)/shard_map/ppermute | solution.py:10
  15.0 25.2 %collective-permute-start.1 = (bf16[64,128]{1,0:T(8,128)(2,1)}, bf16[64,128]{1,0:T(8,128)(2,1)}, u32[]{:S(2)}, u32[]{:S(2)}) collective-permute-start(bf16[64,128]{1,0:T(8,128)(2,1)} %get-tuple-element.128), channel_id=1, source_target_pairs={{1,0},{2,1},{3,2},{5,4},{6,5},{7,6},{9,8},{10,9},{11,10},{13,12},{... | collective-permute-start | bytes 49160 | tf_op jit(solution)/shard_map/ppermute | solution.py:10
  16.9 24.0 %collective-permute-start.2 = (bf16[128,128]{1,0:T(8,128)(2,1)}, bf16[128,128]{1,0:T(8,128)(2,1)}, u32[]{:S(2)}, u32[]{:S(2)}) collective-permute-start(bf16[128,128]{1,0:T(8,128)(2,1)} %get-tuple-element.127), channel_id=1, source_target_pairs={{0,4},{4,8},{8,12},{12,16},{16,20},{20,24},{24,28},{1,5},{5,9},{9,... | collective-permute-start | bytes 98312 | tf_op jit(solution)/shard_map/ppermute | solution.py:10
  21.7 20.0 %collective-permute-start.3 = (bf16[128,128]{1,0:T(8,128)(2,1)}, bf16[128,128]{1,0:T(8,128)(2,1)}, u32[]{:S(2)}, u32[]{:S(2)}) collective-permute-start(bf16[128,128]{1,0:T(8,128)(2,1)} %get-tuple-element.126), channel_id=1, source_target_pairs={{4,0},{8,4},{12,8},{16,12},{20,16},{24,20},{28,24},{5,1},{9,5},{13... | collective-permute-start | bytes 98312 | tf_op jit(solution)/shard_map/ppermute | solution.py:10
  71.3 18.9 %collective-permute-start.6 = (bf16[128,128]{0,1:T(8,128)(2,1)S(1)}, bf16[128,128]{0,1:T(8,128)(2,1)}, u32[]{:S(2)}, u32[]{:S(2)}) collective-permute-start(bf16[128,128]{0,1:T(8,128)(2,1)S(1)} %get-tuple-element.123), channel_id=1, source_target_pairs={{0,4},{4,8},{8,12},{12,16},{16,20},{20,24},{24,28},{1,5},{5,9},{9,... | collective-permute-start | bytes 98312 | tf_op jit(solution)/shard_map/ppermute | solution.py:10
  76.4 14.4 %collective-permute-start.7 = (bf16[128,128]{0,1:T(8,128)(2,1)S(1)}, bf16[128,128]{0,1:T(8,128)(2,1)}, u32[]{:S(2)}, u32[]{:S(2)}) collective-permute-start(bf16[128,128]{0,1:T(8,128)(2,1)S(1)} %get-tuple-element.122), channel_id=1, source_target_pairs={{4,0},{8,4},{12,8},{16,12},{20,16},{24,20},{28,24},{5,1},{9,5},{13... | collective-permute-start | bytes 98312 | tf_op jit(solution)/shard_map/ppermute | solution.py:10
  78.4 11.8 %collective-permute-start.4 = (bf16[64,128]{0,1:T(8,128)(2,1)}, bf16[64,128]{0,1:T(8,128)(2,1)S(1)}, u32[]{:S(2)}, u32[]{:S(2)}) collective-permute-start(bf16[64,128]{0,1:T(8,128)(2,1)} %get-tuple-element.125), channel_id=1, source_target_pairs={{0,1},{1,2},{2,3},{4,5},{5,6},{6,7},{8,9},{9,10},{10,11},{12,13},{... | collective-permute-start | bytes 49160 | tf_op jit(solution)/shard_map/ppermute | solution.py:10
  81.3 8.9 %collective-permute-start.5 = (bf16[64,128]{0,1:T(8,128)(2,1)S(1)}, bf16[64,128]{0,1:T(8,128)(2,1)S(1)}, u32[]{:S(2)}, u32[]{:S(2)}) collective-permute-start(bf16[64,128]{0,1:T(8,128)(2,1)S(1)} %get-tuple-element.124), channel_id=1, source_target_pairs={{1,0},{2,1},{3,2},{5,4},{6,5},{7,6},{9,8},{10,9},{11,10},{13,12},{... | collective-permute-start | bytes 49160 | tf_op jit(solution)/shard_map/ppermute | solution.py:10
  126.1 21.9 %collective-permute-start.8 = (bf16[64,128]{0,1:T(8,128)(2,1)}, bf16[64,128]{0,1:T(8,128)(2,1)}, u32[]{:S(2)}, u32[]{:S(2)}) collective-permute-start(bf16[64,128]{0,1:T(8,128)(2,1)} %get-tuple-element.121), channel_id=1, source_target_pairs={{0,1},{1,2},{2,3},{4,5},{5,6},{6,7},{8,9},{9,10},{10,11},{12,13},{... | collective-permute-start | bytes 49160 | tf_op jit(solution)/shard_map/ppermute | solution.py:10
  131.8 16.2 %collective-permute-start.9 = (bf16[64,128]{0,1:T(8,128)(2,1)}, bf16[64,128]{0,1:T(8,128)(2,1)}, u32[]{:S(2)}, u32[]{:S(2)}) collective-permute-start(bf16[64,128]{0,1:T(8,128)(2,1)} %get-tuple-element.120), channel_id=1, source_target_pairs={{1,0},{2,1},{3,2},{5,4},{6,5},{7,6},{9,8},{10,9},{11,10},{13,12},{... | collective-permute-start | bytes 49160 | tf_op jit(solution)/shard_map/ppermute | solution.py:10
  133.1 14.9 %collective-permute-start.10 = (bf16[128,128]{0,1:T(8,128)(2,1)}, bf16[128,128]{0,1:T(8,128)(2,1)}, u32[]{:S(2)}, u32[]{:S(2)}) collective-permute-start(bf16[128,128]{0,1:T(8,128)(2,1)} %get-tuple-element.119), channel_id=1, source_target_pairs={{0,4},{4,8},{8,12},{12,16},{16,20},{20,24},{24,28},{1,5},{5,9},{9,... | collective-permute-start | bytes 98312 | tf_op jit(solution)/shard_map/ppermute | solution.py:10
  138.2 9.8 %collective-permute-start.11 = (bf16[128,128]{0,1:T(8,128)(2,1)}, bf16[128,128]{0,1:T(8,128)(2,1)}, u32[]{:S(2)}, u32[]{:S(2)}) collective-permute-start(bf16[128,128]{0,1:T(8,128)(2,1)} %get-tuple-element.118), channel_id=1, source_target_pairs={{4,0},{8,4},{12,8},{16,12},{20,16},{24,20},{28,24},{5,1},{9,5},{13... | collective-permute-start | bytes 98312 | tf_op jit(solution)/shard_map/ppermute | solution.py:10
  139.7 44.5 %copy-start.5 = (f32[512,128]{0,1:T(8,128)}, f32[512,128]{0,1:T(8,128)S(1)}, u32[]{:S(2)}) copy-start(f32[512,128]{0,1:T(8,128)S(1)} %copy.137) | copy-start | bytes 786436
  242.6 32.3 %copy-start.19 = (f32[512,128]{0,1:T(8,128)S(1)}, f32[512,128]{0,1:T(8,128)}, u32[]{:S(2)}) copy-start(f32[512,128]{0,1:T(8,128)} %copy-done.18) | copy-start | bytes 786436
  242.6 29.0 %collective-permute-start.15 = (bf16[128,128]{1,0:T(8,128)(2,1)}, bf16[128,128]{1,0:T(8,128)(2,1)S(1)}, u32[]{:S(2)}, u32[]{:S(2)}) collective-permute-start(bf16[128,128]{1,0:T(8,128)(2,1)} %get-tuple-element.117), channel_id=1, source_target_pairs={{4,0},{8,4},{12,8},{16,12},{20,16},{24,20},{28,24},{5,1},{9,5},{13... | collective-permute-start | bytes 98312 | tf_op jit(solution)/shard_map/ppermute | solution.py:10
  244.1 27.5 %collective-permute-start.14 = (bf16[128,128]{1,0:T(8,128)(2,1)S(1)}, bf16[128,128]{1,0:T(8,128)(2,1)S(1)}, u32[]{:S(2)}, u32[]{:S(2)}) collective-permute-start(bf16[128,128]{1,0:T(8,128)(2,1)S(1)} %copy-done.111), channel_id=1, source_target_pairs={{0,4},{4,8},{8,12},{12,16},{16,20},{20,24},{24,28},{1,5},{5,9},{9,... | collective-permute-start | bytes 98312 | tf_op jit(solution)/shard_map/ppermute | solution.py:10
  249.3 22.3 %collective-permute-start.13 = (bf16[64,128]{1,0:T(8,128)(2,1)}, bf16[64,128]{1,0:T(8,128)(2,1)S(1)}, u32[]{:S(2)}, u32[]{:S(2)}) collective-permute-start(bf16[64,128]{1,0:T(8,128)(2,1)} %get-tuple-element.115), channel_id=1, source_target_pairs={{1,0},{2,1},{3,2},{5,4},{6,5},{7,6},{9,8},{10,9},{11,10},{13,12},{... | collective-permute-start | bytes 49160 | tf_op jit(solution)/shard_map/ppermute | solution.py:10
  250.6 21.0 %collective-permute-start.12 = (bf16[64,128]{1,0:T(8,128)(2,1)}, bf16[64,128]{1,0:T(8,128)(2,1)S(1)}, u32[]{:S(2)}, u32[]{:S(2)}) collective-permute-start(bf16[64,128]{1,0:T(8,128)(2,1)} %get-tuple-element.114), channel_id=1, source_target_pairs={{0,1},{1,2},{2,3},{4,5},{5,6},{6,7},{8,9},{9,10},{10,11},{12,13},{... | collective-permute-start | bytes 49160 | tf_op jit(solution)/shard_map/ppermute | solution.py:10
  333.7 36.9 %copy-start.15 = (f32[512,128]{0,1:T(8,128)S(1)}, f32[512,128]{0,1:T(8,128)}, u32[]{:S(2)}) copy-start(f32[512,128]{0,1:T(8,128)} %copy-done.14) | copy-start | bytes 786436
  334.5 36.2 %copy-start.94 = (f32[512]{0:T(512)S(1)}, f32[512]{0:T(512)}, u32[]{:S(2)}) copy-start(f32[512]{0:T(512)} %copy-done.93) | copy-start | bytes 6148
  334.5 36.2 %copy-start.100 = (f32[512]{0:T(512)S(1)}, f32[512]{0:T(512)}, u32[]{:S(2)}) copy-start(f32[512]{0:T(512)} %copy-done.99) | copy-start | bytes 6148
  334.5 36.2 %copy-start.121 = (f32[128]{0:T(128)S(1)}, f32[128]{0:T(128)}, u32[]{:S(2)}) copy-start(f32[128]{0:T(128)} %get-tuple-element.136) | copy-start | bytes 1540
  334.5 30.9 %collective-permute-start.19 = (bf16[128,128]{1,0:T(8,128)(2,1)}, bf16[128,128]{1,0:T(8,128)(2,1)S(1)}, u32[]{:S(2)}, u32[]{:S(2)}) collective-permute-start(bf16[128,128]{1,0:T(8,128)(2,1)} %get-tuple-element.113), channel_id=1, source_target_pairs={{4,0},{8,4},{12,8},{16,12},{20,16},{24,20},{28,24},{5,1},{9,5},{13... | collective-permute-start | bytes 98312 | tf_op jit(solution)/shard_map/ppermute | solution.py:10
  335.9 29.4 %collective-permute-start.18 = (bf16[128,128]{1,0:T(8,128)(2,1)S(1)}, bf16[128,128]{1,0:T(8,128)(2,1)S(1)}, u32[]{:S(2)}, u32[]{:S(2)}) collective-permute-start(bf16[128,128]{1,0:T(8,128)(2,1)S(1)} %copy-done.110), channel_id=1, source_target_pairs={{0,4},{4,8},{8,12},{12,16},{16,20},{20,24},{24,28},{1,5},{5,9},{9,... | collective-permute-start | bytes 98312 | tf_op jit(solution)/shard_map/ppermute | solution.py:10
  341.1 24.2 %collective-permute-start.17 = (bf16[64,128]{1,0:T(8,128)(2,1)}, bf16[64,128]{1,0:T(8,128)(2,1)S(1)}, u32[]{:S(2)}, u32[]{:S(2)}) collective-permute-start(bf16[64,128]{1,0:T(8,128)(2,1)} %get-tuple-element.111), channel_id=1, source_target_pairs={{1,0},{2,1},{3,2},{5,4},{6,5},{7,6},{9,8},{10,9},{11,10},{13,12},{... | collective-permute-start | bytes 49160 | tf_op jit(solution)/shard_map/ppermute | solution.py:10
  342.4 22.9 %collective-permute-start.16 = (bf16[64,128]{1,0:T(8,128)(2,1)}, bf16[64,128]{1,0:T(8,128)(2,1)S(1)}, u32[]{:S(2)}, u32[]{:S(2)}) collective-permute-start(bf16[64,128]{1,0:T(8,128)(2,1)} %get-tuple-element.110), channel_id=1, source_target_pairs={{0,1},{1,2},{2,3},{4,5},{5,6},{6,7},{8,9},{9,10},{10,11},{12,13},{... | collective-permute-start | bytes 49160 | tf_op jit(solution)/shard_map/ppermute | solution.py:10
  426.9 12.8 %collective-permute-start.23 = (bf16[128,128]{1,0:T(8,128)(2,1)S(1)}, bf16[128,128]{1,0:T(8,128)(2,1)S(1)}, u32[]{:S(2)}, u32[]{:S(2)}) collective-permute-start(bf16[128,128]{1,0:T(8,128)(2,1)S(1)} %get-tuple-element.109), channel_id=1, source_target_pairs={{4,0},{8,4},{12,8},{16,12},{20,16},{24,20},{28,24},{5,1},{9,5},{13... | collective-permute-start | bytes 98312 | tf_op jit(solution)/shard_map/ppermute | solution.py:10
  428.2 11.5 %collective-permute-start.22 = (bf16[128,128]{1,0:T(8,128)(2,1)S(1)}, bf16[128,128]{1,0:T(8,128)(2,1)S(1)}, u32[]{:S(2)}, u32[]{:S(2)}) collective-permute-start(bf16[128,128]{1,0:T(8,128)(2,1)S(1)} %get-tuple-element.108), channel_id=1, source_target_pairs={{0,4},{4,8},{8,12},{12,16},{16,20},{20,24},{24,28},{1,5},{5,9},{9,... | collective-permute-start | bytes 98312 | tf_op jit(solution)/shard_map/ppermute | solution.py:10
  433.4 6.3 collective-permute-start.21
  434.7 5.0 collective-permute-start.20
  442.6 337.5 %copy-start.58 = (f32[512,128]{1,0:T(8,128)}, f32[512,128]{1,0:T(8,128)S(1)}, u32[]{:S(2)}) copy-start(f32[512,128]{1,0:T(8,128)S(1)} %scatter_custom_fusion.11) | copy-start | bytes 786436
  (163 other events, 1159.9 us)
Sparse Core Ops, SparseCore 0:
  398.9 359.4 all-gather.3
